TPU v7x, 128 devices: a whole 4x4x4 slice. The times are simulated.
128 devices in a mesh: fit: 16 (over z, x), basis: 4 (over y_hi, core), occ: 2 (over y_lo).
Axes of the slice: x: 4, y: 4 (y_hi: 2, y_lo: 2; y = y_hi * 2 + y_lo), z: 4, core: 2. Of those that a mesh axis runs over, the one named last changes fastest.
Arguments:
- ints: bfloat16 [256, 12288, 128], P('fit', 'basis'), may hold values from -0.5 to 0.5
- coeffs: bfloat16 [12288, 128], P('fit', 'occ'), may hold values from -0.59765625 to 0.59765625
- offsets: int32 [192, 2], P('basis'), may hold values from 0 to 191
- mask: int32 [192, 2], P('basis'), may hold values 0 or 1
Outputs:
- exchange: float32 [12288, 4, 512], P(('fit', 'occ'), None, 'basis')
All inputs are finite; a program needn't handle non-finite values. No bound on the sum of `mask` on one device may be relied on, other than what follows from the above.
Results may differ from a plain program's by a relative error of at most 0.003.
Values may be sent and summed in bfloat16 or wider, within the bound.
A program may use at most 192 MiB of HBM per device.

v0:
```python
import jax
import jax.numpy as jnp
import numpy as np
from jax import lax
from jax.sharding import PartitionSpec as P

BLK = 64
NNZ = 2
MU_DEV = 128


SIGN_ENTRIES = (
    (0, 0, 0, 1),
    (0, 1, 1, 1),
    (0, 2, 2, 1),
    (0, 3, 3, 1),
    (1, 0, 1, -1),
    (1, 1, 0, 1),
    (1, 2, 3, -1),
    (1, 3, 2, 1),
    (2, 0, 2, -1),
    (2, 1, 3, 1),
    (2, 2, 0, 1),
    (2, 3, 1, -1),
    (3, 0, 3, -1),
    (3, 1, 2, -1),
    (3, 2, 1, 1),
    (3, 3, 0, 1),
)


def joined_along(parts, dim):
    parts = jnp.moveaxis(parts, 0, dim)
    shape = parts.shape
    return parts.reshape(*shape[:dim], shape[dim] * shape[dim + 1], *shape[dim + 2 :])


def from_everyone(shard, axis):
    size = lax.axis_size(axis)
    return lax.all_to_all(
        jnp.broadcast_to(shard[None], (size, *shard.shape)), axis, 0, 0, tiled=True
    )


def collect(shard, axis, dim):
    return joined_along(from_everyone(shard, axis), dim)


def split_up(shard, dim, size):
    shape = shard.shape
    parts = shard.reshape(*shape[:dim], size, shape[dim] // size, *shape[dim + 1 :])
    return jnp.moveaxis(parts, dim, 0)


def sum_at_owner(shard, axis, dim):
    parts = split_up(shard, dim, lax.axis_size(axis))
    arrived = lax.all_to_all(parts, axis, split_axis=0, concat_axis=0, tiled=True)
    return arrived.sum(axis=0)


def sign_table():
    table = np.zeros((4, 4, 4), np.float32)
    for entry in SIGN_ENTRIES:
        table[entry[0], entry[1], entry[2]] = entry[3]
    return table


def contract(rows_part, mixed):
    return lax.dot_general(
        rows_part, mixed, (((1,), (1,)), ((), ())), preferred_element_type=jnp.float32
    )


def shards(ints, coeffs, offsets, mask):
    full = collect(coeffs, "fit", 0)
    width = full.shape[1]
    blocks = full.reshape(-1, BLK, width)
    picked = jnp.take(blocks, offsets, axis=0) * mask[:, :, None, None].astype(jnp.bfloat16)
    picked = picked.reshape(offsets.shape[0], NNZ * BLK, width)
    aux_count, rows, stored = ints.shape
    grouped = ints.reshape(aux_count, rows // BLK, BLK, stored)
    half = jnp.einsum("arjk,rkw->rjaw", grouped, picked, preferred_element_type=jnp.float32)
    half = half.reshape(rows, aux_count * width).astype(jnp.bfloat16)
    window = half[:MU_DEV].astype(jnp.float32).reshape(MU_DEV, -1, 4)
    mixed = jnp.einsum("rqs,mkq->rmks", jnp.asarray(sign_table(), jnp.float32), window)
    mixed = mixed.reshape(4 * MU_DEV, -1).astype(jnp.bfloat16)
    terms = contract(lax.all_gather(half, "basis", axis=0, tiled=True), mixed)
    partial_fit = lax.psum_scatter(terms, "fit", scatter_dimension=0, tiled=True)
    result = sum_at_owner(partial_fit, "occ", 0)
    return result.reshape(result.shape[0], 4, MU_DEV)


def solution(mesh):
    return jax.shard_map(
        shards,
        mesh=mesh,
        in_specs=(P("fit", "basis", None), P("fit", "occ"), P("basis", None), P("basis", None)),
        out_specs=P(("fit", "occ"), None, "basis"),
        check_vma=False,
    )
```

profile of v0, /device:TPU:25, one launch (start us, length us, event | category | flops | bytes accessed | tf_op | source)
XLA Modules:
  0.0 461.8 jit_solution(10026369443056584956)
XLA Ops:
  6.5 2.2 broadcast_in_dim.26
  8.7 7.6 %all-to-all-start = ((bf16[16,768,64]{1,2,0:T(8,128)(2,1)}), bf16[16,768,64]{1,2,0:T(8,128)(2,1)}, u32[]{:S(2)}, u32[]{:S(2)}) async-start(bf16[16,768,64]{1,2,0:T(8,128)(2,1)} %broadcast_in_dim.26), calls=%async_computation | async-start | bytes 3145728 | tf_op jit(solution)/shard_map/all_to_all | solution.py:40
  16.4 0.0 all-gather.2.cloned.1.call-start
  16.4 0.7 convert_element_type.23
  17.1 0.1 copy.36
  17.2 0.1 mul.13
  17.3 0.1 mul.14
  17.4 0.7 compare_and_fusion
  18.1 0.1 copy.32
  18.2 0.7 compare_select_fusion
  18.9 0.1 copy.34
  19.0 0.1 reshape.36
  19.2 20.4 %all-to-all-done = bf16[16,768,64]{1,2,0:T(8,128)(2,1)} async-done(((bf16[16,768,64]{1,2,0:T(8,128)(2,1)}), bf16[16,768,64]{1,2,0:T(8,128)(2,1)}, u32[]{:S(2)}, u32[]{:S(2)}) %all-to-all-start) | async-done | bytes 1572896 | tf_op jit(solution)/shard_map/all_to_all | solution.py:40
  39.5 3.1 copy.33
  42.6 2.0 gather_fusion
  44.6 1.8 copy.45
  46.4 0.1 multiply_bitcast_fusion
  46.5 17.7 %convert_bitcast_fusion = bf16[48,64,16,64]{1,3,2,0:T(8,128)(2,1)} fusion(bf16[16,48,64,128]{3,2,1,0:T(8,128)(2,1)} %bitcast.27, bf16[48,128,64,1]{1,0,2,3:T(8,128)(2,1)S(1)} %multiply_bitcast_fusion), kind=kOutput, calls=%fused_computation.3 | convolution fusion | flops 808452096 | bytes 19660800 | tf_op jit(solution)/shard_map/arjk,rkw->rjaw/dot_general | solution.py:82
  64.2 17.5 %copy.39 = bf16[48,64,16,64]{3,2,1,0:T(8,128)(2,1)} copy(bf16[48,64,16,64]{1,3,2,0:T(8,128)(2,1)} %convert_bitcast_fusion) | data formatting | bytes 12582912 | tf_op jit(solution)/shard_map/convert_element_type | solution.py:83
  81.7 0.0 slice-start
  81.7 0.0 copy-start
  81.7 17.3 %convert_element_type.26 = bf16[3072,1024]{1,0:T(8,128)(2,1)} reshape(bf16[48,64,16,64]{3,2,1,0:T(8,128)(2,1)} %copy.39) | data formatting | bytes 12582912 | tf_op jit(solution)/shard_map/convert_element_type | solution.py:83
  99.0 0.0 all-gather.2.cloned.1.call-update
  99.0 0.2 reduce-scatter.2.cloned.1.call-start
  99.3 0.0 slice-done
  99.3 0.5 copy.40
  99.8 0.2 reshape.31
  100.1 0.2 copy.44
  100.3 0.0 copy-done
  100.3 0.7 fusion.4
  101.0 1.8 copy.42
  102.8 152.8 %all-gather.2.cloned.1.call-done = bf16[12288,1024]{1,0:T(8,128)(2,1)} async-done(((bf16[3072,1024]{1,0:T(8,128)(2,1)}), bf16[12288,1024]{1,0:T(8,128)(2,1)}) %all-gather.2.cloned.1.call-update) | async-done | bytes 25165840 | tf_op jit(solution)/shard_map/all_gather | solution.py:87
  255.6 22.5 %fusion.5 = f32[12288,512]{1,0:T(8,128)} fusion(bf16[12288,1024]{1,0:T(8,128)(2,1)} %all-gather.2.cloned.1.call-done, bf16[128,8,4,128]{3,2,1,0:T(4,128)(2,1)S(1)} %bitcast.32), kind=kOutput, calls=%fused_computation.6 | convolution fusion | flops 12884901888 | bytes 51380224 | tf_op jit(solution)/shard_map/dot_general | solution.py:69
  278.1 0.0 reduce-scatter.2.cloned.1.call-update
  278.1 154.0 %reduce-scatter.2.cloned.1.call-done = f32[768,512]{1,0:T(8,128)} async-done(((f32[12288,512]{1,0:T(8,128)}), f32[768,512]{1,0:T(8,128)}) %reduce-scatter.2.cloned.1.call-update) | async-done | bytes 1572880 | tf_op jit(solution)/shard_map/reduce_scatter | solution.py:88
  432.1 21.6 %all_to_all.10 = f32[2,384,512]{2,1,0:T(8,128)S(1)} all-to-all(f32[2,384,512]{2,1,0:T(8,128)} %bitcast.30), channel_id=1, replica_groups=mesh['fit'=16,'basis'=4,'occ'=2] {'occ'}, dimensions={0} | all-to-all | bytes 3145728 | tf_op jit(solution)/shard_map/all_to_all | solution.py:57
  453.7 0.2 reduce_sum.9
  453.9 1.1 reshape.33
  (2 shorter events, 0.0 us)
Async XLA Ops:
  8.7 30.8 %all-to-all-start = ((bf16[16,768,64]{1,2,0:T(8,128)(2,1)}), bf16[16,768,64]{1,2,0:T(8,128)(2,1)}, u32[]{:S(2)}, u32[]{:S(2)}) async-start(bf16[16,768,64]{1,2,0:T(8,128)(2,1)} %broadcast_in_dim.26), calls=%async_computation | async-start | bytes 3145728 | tf_op jit(solution)/shard_map/all_to_all | solution.py:40
  16.4 239.2 %all-gather.2.cloned.1.call-start = ((), (), s32[]{:S(2)}) async-start(), calls=%async_computation.3 | async-start | bytes 31457280 | tf_op jit(solution)/shard_map/all_gather | solution.py:87
  81.7 17.5 %slice-start = ((bf16[48,64,16,64]{1,3,2,0:T(8,128)(2,1)}), bf16[2,64,16,64]{1,3,2,0:T(8,128)(2,1)S(1)}, s32[]{:S(2)}) async-start(bf16[48,64,16,64]{1,3,2,0:T(8,128)(2,1)} %convert_bitcast_fusion), calls=%async_computation.5 | async-start | bytes 1048576 | tf_op jit(solution)/shard_map/slice | solution.py:84
  81.7 18.6 %copy-start = (bf16[4,4,4,1]{1,2,0,3:T(4,128)(2,1)S(1)}, bf16[4,4,4,1]{1,2,0,3:T(4,128)(2,1)}, u32[]{:S(2)}) copy-start(bf16[4,4,4,1]{1,2,0,3:T(4,128)(2,1)} %constant.32) | copy-start | bytes 388
  99.0 333.0 %reduce-scatter.2.cloned.1.call-start = ((), (), s32[]{:S(2)}) async-start(), calls=%async_computation.4 | async-start | bytes 26738688 | tf_op jit(solution)/shard_map/reduce_scatter | solution.py:88
Sparse Core Ops, SparseCore 0:
  99.2 156.4 all-gather.1
  278.3 153.7 reduce-scatter.1
where the time goes:
time: 465 us; the launch traced here: 462 us
  waiting for transfers between devices  327 us (70%)
  local copies, waits for them, and re-layouts  48.5 us (10%)
  matrix products  40.9 us (9%)
  blocking collectives  21.6 us (5%)
  between operations  13.5 us (3%)
  starting transfers between devices  7.91 us (2%)
    reduce_scatter x1, waiting for transfers between devices, shards(): lax.psum_scatter(terms, 'fit', scatter_dimension=0, tiled=True)  154 us
    all_gather x1, waiting for transfers between devices, shards(): terms = contract(lax.all_gather(half, 'basis', axis=0, tiled=True), mixed)  153 us
    convert_element_type x2, local copies, waits for them, and re-layouts, shards(): half = half.reshape(rows, aux_count * width).astype(jnp.bfloat16)  34.8 us
    dot_general x1, matrix products, contract(): lax.dot_general(rows_part, mixed, (((1,), (1,)), ((), ())), preferred_ele...  22.5 us
    all_to_all x1, blocking collectives, sum_at_owner(): lax.all_to_all(parts, axis, split_axis=0, concat_axis=0, tiled=True)  21.6 us
    all_to_all x1, waiting for transfers between devices, from_everyone(): lax.all_to_all(jnp.broadcast_to(shard[None], (size, *shard.shape)), axis,...  20.4 us
    dot_general x1, matrix products, shards(): jnp.einsum('arjk,rkw->rjaw', grouped, picked, preferred_element_type=jnp....  17.7 us
  transfers between devices with their start and end apart: 3, of which 3 were waited for; matrix products, arithmetic and copies ran while one was open for 1% of the time, Pallas kernels for 0%

commit v1 on v0

v1 whole, which is shorter than its diff:
```python
import jax
import jax.numpy as jnp
import numpy as np
from jax import lax
from jax.sharding import PartitionSpec as P

BLK = 64
NNZ = 2
MU_DEV = 128
SIGN_ENTRIES = (
    (0, 0, 0, 1),
    (0, 1, 1, 1),
    (0, 2, 2, 1),
    (0, 3, 3, 1),
    (1, 0, 1, -1),
    (1, 1, 0, 1),
    (1, 2, 3, -1),
    (1, 3, 2, 1),
    (2, 0, 2, -1),
    (2, 1, 3, 1),
    (2, 2, 0, 1),
    (2, 3, 1, -1),
    (3, 0, 3, -1),
    (3, 1, 2, -1),
    (3, 2, 1, 1),
    (3, 3, 0, 1),
)


def signed_permutations(width):
    table = np.zeros((4, width, width), np.float32)
    for r, q, s, sign in SIGN_ENTRIES:
        for i in range(width // 4):
            table[r, 4 * i + q, 4 * i + s] = sign
    return table


def half_rows(ints, picked):
    out = jnp.einsum("arjk,rkw->rjaw", ints, picked, preferred_element_type=jnp.float32)
    rows = out.shape[0] * out.shape[1]
    return out.astype(jnp.bfloat16).reshape(rows, -1)


def shards(ints, coeffs, offsets, mask):
    occ = lax.axis_index("occ")
    gathered = lax.all_gather(coeffs, ("fit", "occ"), axis=0)
    gathered = gathered.reshape(16, 2, *coeffs.shape)
    full = jnp.moveaxis(gathered, 1, 2).reshape(-1, 2 * coeffs.shape[1])
    width = full.shape[1]
    blocks = full.reshape(-1, BLK, width)
    aux, rows, stored = ints.shape
    chunk = rows // 8
    per = chunk // BLK

    def picks(off, msk):
        got = jnp.take(blocks, off, axis=0) * msk[:, :, None, None].astype(jnp.bfloat16)
        return got.reshape(off.shape[0], NNZ * BLK, width)

    nwin = MU_DEV // BLK
    window = half_rows(
        ints[:, :MU_DEV].reshape(aux, nwin, BLK, stored), picks(offsets[:nwin], mask[:nwin])
    )
    windows = lax.all_gather(window, "basis", axis=0, tiled=True)
    table = jnp.asarray(signed_permutations(width), jnp.bfloat16)
    mixed = jnp.einsum(
        "bmak,rks->brmas",
        windows.reshape(4, MU_DEV, aux, width),
        table,
        preferred_element_type=jnp.float32,
    ).astype(jnp.bfloat16)
    mixed = mixed.reshape(4, 4 * MU_DEV, aux * width)

    mine = lax.dynamic_index_in_dim(ints.reshape(aux, 4, 2, chunk, stored), occ, 2, False)
    off = lax.dynamic_index_in_dim(offsets.reshape(4, 2, per, NNZ), occ, 1, False)
    msk = lax.dynamic_index_in_dim(mask.reshape(4, 2, per, NNZ), occ, 1, False)
    half = half_rows(
        mine.reshape(aux, 4 * per, BLK, stored),
        picks(off.reshape(4 * per, NNZ), msk.reshape(4 * per, NNZ)),
    )
    terms = jnp.stack(
        [
            lax.dot_general(
                half, mixed[b], (((1,), (1,)), ((), ())), preferred_element_type=jnp.float32
            )
            for b in range(4)
        ]
    )
    terms = terms.reshape(16 * chunk, 4 * MU_DEV)
    summed = lax.psum_scatter(terms, "fit", scatter_dimension=0, tiled=True)
    moves = []
    for z in range(4):
        for x in range(4):
            for b in range(4):
                moves.append(((z * 4 + x) * 4 + b, (b * 4 + x) * 4 + z))
    result = lax.ppermute(summed, ("fit", "basis"), moves)
    return result.reshape(chunk, 4, MU_DEV)


def solution(mesh):
    return jax.shard_map(
        shards,
        mesh=mesh,
        in_specs=(P("fit", "basis", None), P("fit", "occ"), P("basis", None), P("basis", None)),
        out_specs=P(("fit", "occ"), None, "basis"),
        check_vma=False,
    )
```

time: 465 us -> 385 us (0.83)
  waiting for transfers between devices: 327 us -> 269 us
  blocking collectives: 21.6 us -> 0 us
  matrix products: 40.9 us -> 22.5 us
  local copies, waits for them, and re-layouts: 48.5 us -> 57.3 us
  other arithmetic: 2.33 us -> 10 us
    reduce_scatter x1, waiting for transfers between devices: 154 us -> 95.3 us  [shards(): summed = lax.psum_scatter(terms, 'fit', scatter_dimension=0, tiled=True)]
    convert_element_type x4, local copies, waits for them, and re-layouts: 36.7 us -> 8.93 us  [the longest x2 8.75 us: half_rows(): return out.astype(jnp.bfloat16).reshape(rows, -1)]
    all_to_all x1 -> x0, blocking collectives: 21.6 us -> none  [sum_at_owner(): lax.all_to_all(parts, axis, split_axis=0, concat_axis=0, tiled=True)]
    all_to_all x1 -> x0, waiting for transfers between devices: 20.4 us -> none  [from_everyone(): lax.all_to_all(jnp.broadcast_to(shard[None], (size, *shard.shape)), axis,...]
    ppermute x0 -> x1, waiting for transfers between devices: none -> 19.6 us  [shards(): result = lax.ppermute(summed, ('fit', 'basis'), moves)]
    dot_general x3 -> x7, matrix products: 40.9 us -> 22.5 us  [the longest x4 14.2 us: shards(): lax.dot_general(half, mixed[b], (((1,), (1,)), ((), ())), preferred_eleme...]
    another operation x0 -> x2, local copies, waits for them, and re-layouts: none -> 16.9 us  [shards(): blocks = full.reshape(-1, BLK, width)]
    slice x3 -> x7, local copies, waits for them, and re-layouts: 0.55 us -> 8.78 us  [the longest x5 6.79 us: shards(): mixed[b]]
  transfers between devices with their start and end apart: 3 -> 4, of which waited for: 3 -> 4; matrix products, arithmetic and copies ran while one was open for 1% -> 8% of each run, Pallas kernels for 0% -> 0%
where the time goes in v1:
time: 385 us; the launch traced here: 378 us
  waiting for transfers between devices  269 us (70%)
  local copies, waits for them, and re-layouts  57.3 us (15%)
  matrix products  22.5 us (6%)
  between operations  13.8 us (4%)
  other arithmetic  10 us (3%)
  starting transfers between devices  5.44 us (1%)
    all_gather x1, waiting for transfers between devices, shards(): gathered = lax.all_gather(coeffs, ('fit', 'occ'), axis=0)  133 us
    reduce_scatter x1, waiting for transfers between devices, shards(): summed = lax.psum_scatter(terms, 'fit', scatter_dimension=0, tiled=True)  95.3 us
    all_gather x1, waiting for transfers between devices, shards(): windows = lax.all_gather(window, 'basis', axis=0, tiled=True)  20.7 us
    ppermute x1, waiting for transfers between devices, shards(): result = lax.ppermute(summed, ('fit', 'basis'), moves)  19.6 us
    another operation x2, local copies, waits for them, and re-layouts, shards(): blocks = full.reshape(-1, BLK, width)  16.9 us
    dot_general x4, matrix products, shards(): lax.dot_general(half, mixed[b], (((1,), (1,)), ((), ())), preferred_eleme...  14.2 us
    convert_element_type x2, local copies, waits for them, and re-layouts, half_rows(): return out.astype(jnp.bfloat16).reshape(rows, -1)  8.75 us
  transfers between devices with their start and end apart: 4, of which 4 were waited for; matrix products, arithmetic and copies ran while one was open for 8% of the time, Pallas kernels for 0%

profile of v1, /device:TPU:25, one launch (start us, length us, event | category | flops | bytes accessed | tf_op | source)
XLA Modules:
  0.0 378.2 jit_solution(6559923245121987676)
XLA Ops:
  6.5 0.7 all-gather.6.cloned.1.call-update
  7.3 0.7 convert.3
  8.0 0.1 copy.40
  8.3 0.7 compare_and_fusion
  8.9 0.1 copy.37
  9.2 0.7 compare_select_fusion
  9.9 0.1 copy.38
  10.1 1.9 slice.28
  12.0 132.8 %all-gather.6.cloned.1.call-done = bf16[24576,64]{0,1:T(8,128)(2,1)} async-done(((bf16[768,64]{0,1:T(8,128)(2,1)}), bf16[24576,64]{0,1:T(8,128)(2,1)}) %all-gather.6.cloned.1.call-update) | async-done | bytes 3145744 | tf_op jit(solution)/shard_map/all_gather | solution.py:46
  144.8 4.1 %reshape.109 = bf16[16,2,768,64]{2,1,0,3:T(2,128)(2,1)S(1)} reshape(bf16[24576,64]{0,1:T(8,128)(2,1)} %all-gather.6.cloned.1.call-done) | data formatting | bytes 6291456 | tf_op jit(solution)/shard_map/reshape | solution.py:47
  148.9 2.2 copy.111
  151.1 9.0 %reshape_reshape.3 = bf16[192,64,128]{1,0,2:T(8,128)(2,1)} reshape(bf16[16,768,2,64]{1,0,3,2:T(8,128)(2,1)} %bitcast.118) | data formatting | bytes 6291456 | tf_op jit(solution)/shard_map/reshape;reshape | solution.py:50
  160.1 7.9 %copy.33 = bf16[192,64,128]{2,1,0:T(8,128)(2,1)S(1)} copy(bf16[192,64,128]{1,0,2:T(8,128)(2,1)} %reshape_reshape.3) | data formatting | bytes 6291456 | tf_op jit(solution)/shard_map/reshape;reshape | solution.py:50
  168.1 0.6 gather_fusion.1
  168.6 0.1 fusion.42
  168.8 1.3 fusion.37
  170.1 0.3 copy.42
  170.5 1.0 copy.112
  171.8 0.1 copy.34
  172.1 0.5 broadcast.60
  172.6 0.7 fusion.43
  173.5 0.1 copy.30
  173.6 0.1 broadcast_in_dim.31
  173.9 0.1 reshape.122
  174.0 6.2 %constant_dynamic-slice_fusion = bf16[16,4,1,384,128]{4,3,2,1,0:T(8,128)(2,1)} fusion(bf16[16,4,2,384,128]{4,3,2,1,0:T(8,128)(2,1)} %bitcast.126, s32[]{:T(128)S(6)} %select_n.38), kind=kLoop, calls=%fused_computation.52 | loop fusion | bytes 12582916 | tf_op jit(solution)/shard_map/jit(dynamic_index_in_dim)/dynamic_slice | solution.py:73
  180.2 1.6 gather_fusion
  181.7 2.7 fusion.39
  184.5 4.6 %convert_bitcast_fusion.1 = bf16[24,64,16,128]{3,1,2,0:T(8,128)(2,1)S(1)} fusion(bf16[16,24,64,128]{3,2,1,0:T(8,128)(2,1)} %bitcast.117, bf16[24,128,128]{2,1,0:T(8,128)(2,1)S(1)} %fusion.39), kind=kOutput, calls=%fused_computation.14 | convolution fusion | flops 808452096 | bytes 13369344 | tf_op jit(solution)/shard_map/arjk,rkw->rjaw/dot_general | solution.py:39
  189.1 8.4 %copy.36 = bf16[24,64,16,128]{3,2,1,0:T(8,128)(2,1)} copy(bf16[24,64,16,128]{3,1,2,0:T(8,128)(2,1)S(1)} %convert_bitcast_fusion.1) | data formatting | bytes 12582912 | tf_op jit(solution)/shard_map/convert_element_type | solution.py:41
  197.5 20.7 %all-gather.4.cloned.1.call-done = bf16[512,2048]{1,0:T(8,128)(2,1)} async-done(((bf16[128,2048]{1,0:T(8,128)(2,1)}), bf16[512,2048]{1,0:T(8,128)(2,1)}) %all-gather.4.cloned.1.call-update) | async-done | bytes 2097168 | tf_op jit(solution)/shard_map/all_gather | solution.py:63
  218.2 2.2 copy.56
  220.4 0.4 bitcast_bitcast_fusion
  220.8 0.5 copy-done
  221.3 2.3 convert_bitcast_fusion
  223.6 1.4 fusion.44
  225.0 1.4 copy.44
  226.4 1.4 copy.47
  227.8 3.5 fusion.16
  231.3 3.5 fusion.25
  234.8 1.4 copy.46
  236.1 3.8 fusion.22
  239.9 1.4 copy.45
  241.2 3.5 fusion.19
  244.7 5.0 %pad_maximum_fusion = f32[4,1536,512]{2,1,0:T(8,128)} fusion(f32[1,1536,512]{2,1,0:T(8,128)S(1)} %fusion.25, f32[1,1536,512]{2,1,0:T(8,128)S(1)} %fusion.22, f32[1,1536,512]{2,1,0:T(8,128)S(1)} %fusion.19, f32[1,1536,512]{2,1,0:T(8,128)S(1)} %fusion.16), kind=kLoop, calls=%fused_computation.2 | loop fusion | flops 9437184 | bytes 25165824 | tf_op jit(solution)/shard_map/stack | solution.py:80
  249.8 95.3 %reduce-scatter.2.cloned.1.call-done = f32[384,512]{1,0:T(8,128)} async-done(((f32[6144,512]{1,0:T(8,128)}), f32[384,512]{1,0:T(8,128)}) %reduce-scatter.2.cloned.1.call-update) | async-done | bytes 786448 | tf_op jit(solution)/shard_map/reduce_scatter | solution.py:89
  345.1 5.4 %collective-permute-start = (f32[384,512]{1,0:T(8,128)}, f32[384,512]{1,0:T(8,128)S(1)}, u32[]{:S(2)}, u32[]{:S(2)}) collective-permute-start(f32[384,512]{1,0:T(8,128)} %reduce-scatter.2.cloned.1.call-done), channel_id=1, source_target_pairs={{0,0},{2,32},{4,64},{6,96},{8,8},{10,40},{12,72},{14,104},{16,16},... | collective-permute-start | bytes 2359304 | tf_op jit(solution)/shard_map/ppermute | solution.py:95
  350.5 19.6 %collective-permute-done = f32[384,512]{1,0:T(8,128)S(1)} collective-permute-done((f32[384,512]{1,0:T(8,128)}, f32[384,512]{1,0:T(8,128)S(1)}, u32[]{:S(2)}, u32[]{:S(2)}) %collective-permute-start) | collective-permute-done | bytes 786464 | tf_op jit(solution)/shard_map/ppermute | solution.py:95
  370.1 1.1 reshape.119
  (34 shorter events, 1.4 us)
Async XLA Ops:
  6.5 138.3 %all-gather.6.cloned.1.call-start = ((), (), s32[]{:S(2)}) async-start(), calls=%async_computation.3 | async-start | bytes 3244032 | tf_op jit(solution)/shard_map/all_gather | solution.py:46
  7.3 210.9 %all-gather.4.cloned.1.call-start = ((), (), s32[]{:S(2)}) async-start(), calls=%async_computation.1 | async-start | bytes 2621440 | tf_op jit(solution)/shard_map/all_gather | solution.py:63
  168.0 3.5 copy-start.2
  168.1 3.6 copy-start.1
  171.5 173.7 %reduce-scatter.2.cloned.1.call-start = ((), (), s32[]{:S(2)}) async-start(), calls=%async_computation.2 | async-start | bytes 13369344 | tf_op jit(solution)/shard_map/reduce_scatter | solution.py:89
  220.4 0.9 copy-start
  221.3 6.4 %slice-start = ((s8[6291456]{0:T(1024)(128)(4,1)}), s8[2097152]{0:T(1024)(128)(4,1)S(1)}, s32[]{:S(2)}) async-start(s8[6291456]{0:T(1024)(128)(4,1)} %bitcast.120), calls=%async_computation.4 | async-start | bytes 4194304
  223.6 4.1 %slice-start.1 = ((s8[6291456]{0:T(1024)(128)(4,1)}), s8[4194304]{0:T(1024)(128)(4,1)S(1)}, s32[]{:S(2)}) async-start(s8[6291456]{0:T(1024)(128)(4,1)} %bitcast.120), calls=%async_computation.5 | async-start | bytes 8388608
  345.1 25.0 %collective-permute-start = (f32[384,512]{1,0:T(8,128)}, f32[384,512]{1,0:T(8,128)S(1)}, u32[]{:S(2)}, u32[]{:S(2)}) collective-permute-start(f32[384,512]{1,0:T(8,128)} %reduce-scatter.2.cloned.1.call-done), channel_id=1, source_target_pairs={{0,0},{2,32},{4,64},{6,96},{8,8},{10,40},{12,72},{14,104},{16,16},... | collective-permute-start | bytes 2359304 | tf_op jit(solution)/shard_map/ppermute | solution.py:95
Sparse Core Ops, SparseCore 0:
  9.0 135.7 all-gather.5
  171.6 46.5 all-gather.3
  249.9 95.1 reduce-scatter.1

commit v2 on v0

v2 whole, which is shorter than its diff:
```python
import functools

import jax
import jax.numpy as jnp
import numpy as np
from jax import lax
from jax.experimental import pallas as pl
from jax.experimental.pallas import tpu as pltpu
from jax.sharding import PartitionSpec as P

BLK = 64
NNZ = 2
MU_DEV = 128
AUX = 16
ROWS = 3072
CHUNK = 384
QUART = 96
WIDTH = 128
KDIM = AUX * WIDTH
MESH = pl.DeviceIdType.MESH
SIGN_ENTRIES = (
    (0, 0, 0, 1),
    (0, 1, 1, 1),
    (0, 2, 2, 1),
    (0, 3, 3, 1),
    (1, 0, 1, -1),
    (1, 1, 0, 1),
    (1, 2, 3, -1),
    (1, 3, 2, 1),
    (2, 0, 2, -1),
    (2, 1, 3, 1),
    (2, 2, 0, 1),
    (2, 3, 1, -1),
    (3, 0, 3, -1),
    (3, 1, 2, -1),
    (3, 2, 1, 1),
    (3, 3, 0, 1),
)


def signed_permutations():
    table = np.zeros((WIDTH, 4, WIDTH), np.float32)
    for r, q, s, sign in SIGN_ENTRIES:
        for i in range(WIDTH // 4):
            table[4 * i + q, r, 4 * i + s] = sign
    return table.reshape(WIDTH, 4 * WIDTH)


def dot_nt(a, b):
    return lax.dot_general(
        a, b, (((1,), (1,)), ((), ())), preferred_element_type=jnp.float32
    )


def kernel(
    ints, coef, table, offs, mask, out,
    win_in, ints_v, G, win, mixed, half, part,
    r1a, r1b, r2a, r2b, q1, q2, fin,
    lsem, gs, gr, ws, wr, s1s, s1r, s2s, s2r, ts, tr,
):
    fit = lax.axis_index("fit")
    b = lax.axis_index("basis")
    yl = lax.axis_index("occ")
    z = fit // 4
    x = fit % 4
    yh = b // 2
    c = b % 2
    oyl = 1 - yl
    partner = 2 * yh + (1 - c)

    def basis_at(k):
        return 2 * ((yh + k // 2) % 2) + (c + k % 2) % 2

    def dev(zz, xx, bb, ll):
        return (zz * 4 + xx, bb, ll)

    def rows(q):
        return pl.ds(pl.multiple_of(q * QUART, QUART), QUART)

    locals_ = [pltpu.make_async_copy(ints.at[:, pl.ds(0, MU_DEV), :], win_in, lsem.at[0])]
    for xx in range(4):
        start = pl.multiple_of((2 * xx + yl) * CHUNK, CHUNK)
        locals_.append(
            pltpu.make_async_copy(
                ints.at[:, pl.ds(start, CHUNK), :], ints_v.at[xx], lsem.at[1 + xx]
            )
        )
    for copy in locals_:
        copy.start()

    for t in range(3):
        G[z, x, yl, c, t] = coef[:, pl.ds(pl.multiple_of(c * CHUNK + t * 128, 128), 128)]

    barrier = pltpu.get_barrier_semaphore()

    def greet(target):
        pl.semaphore_signal(barrier, inc=1, device_id=target, device_id_type=MESH)

    for dz in range(4):
        for k in range(4):
            if dz or k:
                greet(dev((z + dz) % 4, x, basis_at(k), yl))
    for d in (1, 2, 3):
        greet(dev(z, (x + d) % 4, b, yl))
    greet(dev(z, x, b, oyl))
    greet(dev(z, x, basis_at(2), oyl))
    pl.semaphore_wait(barrier, 20)

    def send(src, dst, ssem, rsem, target):
        copy = pltpu.make_async_remote_copy(
            src_ref=src,
            dst_ref=dst,
            send_sem=ssem,
            recv_sem=rsem,
            device_id=target,
            device_id_type=MESH,
        )
        copy.start()
        return copy

    sent = []


    def gather(src, dst, n, target):
        copy = send(src, dst, gs.at[n], gr.at[n], target)
        sent.append(copy)
        return copy

    mine = G.at[z, x, yl, c]
    first = gather(mine, mine, 0, dev(z, x, b, oyl))
    first.wait_recv()
    along_x = []
    along_z = []
    ga = G.at[z, x, 0, c]
    gb = G.at[z, x, 1, c]
    for d in (1, 3, 2):
        along_x.append(gather(ga, ga, d, dev(z, (x + d) % 4, b, yl)))
        along_z.append(gather(gb, gb, 3 + d, dev((z + d) % 4, x, b, yl)))
    for one, two in zip(along_x, along_z):
        one.wait_recv()
        two.wait_recv()
    zp, zm, z2 = (z + 1) % 4, (z + 3) % 4, (z + 2) % 4
    xp, xm, x2 = (x + 1) % 4, (x + 3) % 4, (x + 2) % 4
    onchip = []

    def group(color, at):
        return G.at[at, :, 0, c] if color == 0 else G.at[:, at, 1, c]

    def pair(color, at, n):
        ref = group(color, at)
        onchip.append(gather(ref, ref, n, dev(z, x, partner, yl)))

    up = (dev(zp, x, b, yl), dev(z, xp, b, yl))
    down = (dev(zm, x, b, yl), dev(z, xm, b, yl))
    here = (z, x)
    above = (zp, xp)
    below = (zm, xm)
    far = (z2, x2)
    ups, downs = [], []
    for color in range(2):
        ref = group(color, here[color])
        ups.append(gather(ref, ref, 7 + color, up[color]))
        downs.append(gather(ref, ref, 9 + color, down[color]))
    for color in range(2):
        pair(color, here[color], 15 + color)
    fars = []
    for color in range(2):
        ups[color].wait_recv()
        ref = group(color, below[color]).at[:, :, pl.ds(0, 32), :]
        fars.append(gather(ref, ref, 11 + color, up[color]))
        downs[color].wait_recv()
        ref = group(color, above[color]).at[:, :, pl.ds(32, 32), :]
        fars.append(gather(ref, ref, 13 + color, down[color]))
        pair(color, below[color], 17 + color)
        pair(color, above[color], 19 + color)
    for copy in fars:
        copy.wait_recv()
    for color in range(2):
        pair(color, far[color], 21 + color)
    for copy in onchip:
        copy.wait_recv()

    lane = lax.broadcasted_iota(jnp.int32, (WIDTH, WIDTH), 1)

    def picked(rb):
        sides = []
        for k in range(NNZ):
            off = offs[k, rb]
            keep = mask[k, rb].astype(jnp.float32)
            odd = lax.rem(off, 2).astype(jnp.float32) * keep
            even = keep - odd
            tile = lax.div(off, 2)
            f = lax.div(tile, 6)
            core = lax.div(lax.rem(tile, 6), 3)
            at = (lax.div(f, 4), lax.rem(f, 4))
            got = jnp.concatenate(
                [G[(*at, o, core, lax.rem(tile, 3))] for o in range(2)], axis=0
            ).astype(jnp.float32)
            turned = pltpu.roll(got, 64, 1)
            if k == 0:
                sides.append(got * even + turned * odd)
            else:
                sides.append(got * odd + turned * even)
        return jnp.where(lane < BLK, sides[0], sides[1]).astype(jnp.bfloat16)

    locals_[0].wait()
    for rb in range(MU_DEV // BLK):
        slab = win_in[:, rb * BLK : (rb + 1) * BLK, :].reshape(AUX * BLK, WIDTH)
        got = dot_nt(slab, picked(rb)).astype(jnp.bfloat16)
        for p in range(AUX):
            win[b, rb * BLK : (rb + 1) * BLK, p * WIDTH : (p + 1) * WIDTH] = got[
                p * BLK : (p + 1) * BLK
            ]
    window = [
        send(win.at[b], win.at[b], ws.at[0], wr.at[0], dev(z, x, partner, yl)),
        send(win.at[b], win.at[b], ws.at[1], wr.at[1], dev(z, x, basis_at(2), oyl)),
    ]
    sent.extend(window)

    for xx in range(4):
        locals_[1 + xx].wait()

    @pl.loop(0, 24)
    def _(i):
        xx = i // 6
        r = i % 6
        slab = ints_v[xx, :, pl.ds(pl.multiple_of(r * BLK, BLK), BLK), :]
        weights = picked((2 * xx + yl) * 6 + r)
        got = dot_nt(slab.reshape(AUX * BLK, WIDTH), weights).astype(jnp.bfloat16)
        at = pl.ds(pl.multiple_of(i * BLK, BLK), BLK)
        for p in range(AUX):
            half[at, p * WIDTH : (p + 1) * WIDTH] = got[p * BLK : (p + 1) * BLK]

    def dots(k):
        bb = basis_at(k)

        @pl.loop(0, AUX)
        def _(p):
            at = pl.ds(pl.multiple_of(p * WIDTH, WIDTH), WIDTH)
            got = jnp.dot(win[bb, :, at], table[...], preferred_element_type=jnp.float32)
            got = got.astype(jnp.bfloat16)
            for r in range(4):
                mixed[r // 2, (r % 2) * 128 : (r % 2) * 128 + 128, at] = got[
                    :, r * WIDTH : (r + 1) * WIDTH
                ]

        @pl.loop(0, 8)
        def _(i):
            h = i // 4
            xx = i % 4
            at = pl.ds(pl.multiple_of(xx * CHUNK, CHUNK), CHUNK)
            part[k, h, xx] = dot_nt(half[at, :], mixed[h]).astype(jnp.bfloat16)

    def chunk_at(k, h, stage, q):
        if k % 2 == 0:
            if stage == 0:
                return part.at[k, h, q]
            return part.at[k, h, x, rows(q)]
        if stage == 0:
            return part.at[k, h, :, rows(q)]
        return part.at[k, h, q, rows(z)]

    def recv_one(k, stage, side):
        if stage:
            return q1.at[k, side]
        return r1a.at[k // 2, side] if k % 2 == 0 else r1b.at[k // 2, side]

    def recv_two(k, stage, side, h):
        if stage:
            return q2.at[k, side, h]
        return r2a.at[k // 2, side, h] if k % 2 == 0 else r2b.at[k // 2, side, h]

    flights = {}

    def ring(k, stage):
        color = (k + stage) % 2
        if color == 0:
            return x, dev(z, xp, b, yl), dev(z, xm, b, yl)
        return z, dev(zp, x, b, yl), dev(zm, x, b, yl)

    def launch(k, stage):
        me, plus, minus = ring(k, stage)
        n = k * 2 + stage
        two = (me + 2) % 4
        nxt, prv = (me + 1) % 4, (me + 3) % 4
        got = {}
        for side, target in ((0, plus), (1, minus)):
            got["one", side] = send(
                chunk_at(k, side, stage, two), recv_one(k, stage, side),
                s1s.at[n, side], s1r.at[n, side], target,
            )
        got["two", 0, 1] = send(
            chunk_at(k, 1, stage, nxt), recv_two(k, stage, 0, 1),
            s2s.at[n, 0, 1], s2r.at[n, 0, 1], plus,
        )
        got["two", 1, 0] = send(
            chunk_at(k, 0, stage, prv), recv_two(k, stage, 1, 0),
            s2s.at[n, 1, 0], s2r.at[n, 1, 0], minus,
        )
        flights[k, stage] = got

    def relay(k, stage):
        me, plus, minus = ring(k, stage)
        n = k * 2 + stage
        got = flights[k, stage]
        for side, target in ((0, plus), (1, minus)):
            got["one", side].wait_recv()
            at = (me + 1) % 4 if side == 0 else (me + 3) % 4
            ref = chunk_at(k, side, stage, at)
            total = ref[...].astype(jnp.float32)
            total += recv_one(k, stage, side)[...].astype(jnp.float32)
            ref[...] = total.astype(jnp.bfloat16)
            got["two", side, side] = send(
                chunk_at(k, side, stage, at), recv_two(k, stage, side, side),
                s2s.at[n, side, side], s2r.at[n, side, side], target,
            )

    def collect(k, stage):
        me, plus, minus = ring(k, stage)
        got = flights[k, stage]
        for h in range(2):
            got["two", 0, h].wait_recv()
            got["two", 1, h].wait_recv()
            ref = chunk_at(k, h, stage, me)
            total = ref[...].astype(jnp.float32)
            total += recv_two(k, stage, 0, h)[...].astype(jnp.float32)
            total += recv_two(k, stage, 1, h)[...].astype(jnp.float32)
            if stage == 0:
                ref[...] = total.astype(jnp.bfloat16)
            else:
                fin[k, :, h * 256 : (h + 1) * 256] = total

    finals = []

    def deliver(k):
        target = dev(b, x, basis_at(k), yl)
        if k == 0:
            same = z == b

            @pl.when(same)
            def _():
                pltpu.make_async_copy(fin.at[k], out.at[z], tr.at[z]).start()

            @pl.when(jnp.logical_not(same))
            def _():
                send(fin.at[k], out.at[z], ts.at[k], tr.at[z], target)
        else:
            finals.append(send(fin.at[k], out.at[z], ts.at[k], tr.at[z], target))

    dots(0)
    launch(0, 0)
    window[0].wait_recv()
    dots(1)
    launch(1, 0)
    window[1].wait_recv()
    other = win.at[basis_at(2)]
    forward = send(other, other, ws.at[2], wr.at[2], dev(z, x, partner, yl))
    sent.append(forward)
    relay(0, 0)
    dots(2)
    launch(2, 0)
    relay(1, 0)
    forward.wait_recv()
    dots(3)
    launch(3, 0)
    collect(0, 0)
    launch(0, 1)
    relay(2, 0)
    collect(1, 0)
    launch(1, 1)
    relay(3, 0)
    relay(0, 1)
    relay(1, 1)
    collect(0, 1)
    deliver(0)
    collect(1, 1)
    deliver(1)
    collect(2, 0)
    launch(2, 1)
    collect(3, 0)
    launch(3, 1)
    relay(2, 1)
    relay(3, 1)
    collect(2, 1)
    deliver(2)
    collect(3, 1)
    deliver(3)

    for q in range(4):
        pltpu.make_async_copy(fin.at[0], out.at[q], tr.at[q]).wait()
    for copy in sent:
        copy.wait_send()
    for got in flights.values():
        for copy in got.values():
            copy.wait_send()

    @pl.when(z != b)
    def _():
        pltpu.make_async_remote_copy(
            src_ref=fin.at[0], dst_ref=out.at[z], send_sem=ts.at[0], recv_sem=tr.at[z],
            device_id=dev(b, x, b, yl), device_id_type=MESH,
        ).wait_send()

    for copy in finals:
        copy.wait_send()


def shards(ints, coeffs, offsets, mask):
    table = jnp.asarray(signed_permutations(), jnp.bfloat16)
    bf16, f32 = jnp.bfloat16, jnp.float32
    vmem = pl.BlockSpec(memory_space=pltpu.VMEM)
    smem = pl.BlockSpec(memory_space=pltpu.SMEM)
    dma = pltpu.SemaphoreType.DMA
    result = pl.pallas_call(
        kernel,
        out_shape=jax.ShapeDtypeStruct((4, QUART, 512), f32),
        in_specs=[pl.BlockSpec(memory_space=pl.ANY), vmem, vmem, smem, smem],
        out_specs=vmem,
        scratch_shapes=[
            pltpu.VMEM((AUX, MU_DEV, WIDTH), bf16),
            pltpu.VMEM((4, AUX, CHUNK, WIDTH), bf16),
            pltpu.VMEM((4, 4, 2, 2, 3, 64, 128), bf16),
            pltpu.VMEM((4, MU_DEV, KDIM), bf16),
            pltpu.VMEM((2, 256, KDIM), bf16),
            pltpu.VMEM((4 * CHUNK, KDIM), bf16),
            pltpu.VMEM((4, 2, 4, CHUNK, 256), bf16),
            pltpu.VMEM((2, 2, CHUNK, 256), bf16),
            pltpu.VMEM((2, 2, 4, QUART, 256), bf16),
            pltpu.VMEM((2, 2, 2, CHUNK, 256), bf16),
            pltpu.VMEM((2, 2, 2, 4, QUART, 256), bf16),
            pltpu.VMEM((4, 2, QUART, 256), bf16),
            pltpu.VMEM((4, 2, 2, QUART, 256), bf16),
            pltpu.VMEM((4, QUART, 512), f32),
            dma((5,)),
            dma((23,)),
            dma((23,)),
            dma((3,)),
            dma((3,)),
            dma((8, 2)),
            dma((8, 2)),
            dma((8, 2, 2)),
            dma((8, 2, 2)),
            dma((4,)),
            dma((4,)),
        ],
        compiler_params=pltpu.CompilerParams(
            collective_id=0, has_side_effects=True, vmem_limit_bytes=60 * 1024 * 1024
        ),
        name="exchange",
    )(ints, coeffs.T, table, offsets.T, mask.T)
    return result.reshape(CHUNK, 4, MU_DEV)


def solution(mesh):
    return jax.shard_map(
        shards,
        mesh=mesh,
        in_specs=(P("fit", "basis", None), P("fit", "occ"), P("basis", None), P("basis", None)),
        out_specs=P(("fit", "occ"), None, "basis"),
        check_vma=False,
    )
```

time: 465 us -> 118 us (0.25)
  waiting for transfers between devices: 327 us -> 0 us
  Pallas kernels: 0 us -> 116 us
  local copies, waits for them, and re-layouts: 48.5 us -> 2.27 us
  matrix products: 40.9 us -> 0 us
  blocking collectives: 21.6 us -> 0 us
  between operations: 13.5 us -> 0.01 us
  starting transfers between devices: 7.91 us -> 0 us
    reduce_scatter x1 -> x0, waiting for transfers between devices: 154 us -> none  [shards(): lax.psum_scatter(terms, 'fit', scatter_dimension=0, tiled=True)]
    all_gather x1 -> x0, waiting for transfers between devices: 153 us -> none  [shards(): terms = contract(lax.all_gather(half, 'basis', axis=0, tiled=True), mixed)]
    pallas_call x0 -> x1, Pallas kernels: none -> 116 us  [shards(): pl.pallas_call(kernel, out_shape=jax.ShapeDtypeStruct((4, QUART, 512), f3...]
    dot_general x3 -> x0, matrix products: 40.9 us -> none  [the longest x1 22.5 us: contract(): lax.dot_general(rows_part, mixed, (((1,), (1,)), ((), ())), preferred_ele...]
    convert_element_type x4 -> x0, local copies, waits for them, and re-layouts: 36.7 us -> none  [the longest x2 34.8 us: shards(): half = half.reshape(rows, aux_count * width).astype(jnp.bfloat16)]
    all_to_all x1 -> x0, blocking collectives: 21.6 us -> none  [sum_at_owner(): lax.all_to_all(parts, axis, split_axis=0, concat_axis=0, tiled=True)]
    all_to_all x1 -> x0, waiting for transfers between devices: 20.4 us -> none  [from_everyone(): lax.all_to_all(jnp.broadcast_to(shard[None], (size, *shard.shape)), axis,...]
    all_to_all x1 -> x0, starting transfers between devices: 7.64 us -> none  [from_everyone(): lax.all_to_all(jnp.broadcast_to(shard[None], (size, *shard.shape)), axis,...]
  transfers between devices with their start and end apart: 3 -> 0, of which waited for: 3 -> 0; matrix products, arithmetic and copies ran while one was open for 1% -> 0% of each run, Pallas kernels for 0% -> 0%
where the time goes in v2:
time: 118 us
  Pallas kernels  116 us (98%)
  local copies, waits for them, and re-layouts  2.27 us (2%)
    pallas_call x1, Pallas kernels, shards(): pl.pallas_call(kernel, out_shape=jax.ShapeDtypeStruct((4, QUART, 512), f3...  116 us

profile of v2, /device:TPU:25, one launch (start us, length us, event | category | flops | bytes accessed | tf_op | source)
XLA Modules:
  0.0 118.2 jit_solution(9032997252949351163)
XLA Ops:
  0.0 116.0 %exchange.1 = f32[4,96,512]{2,1,0:T(8,128)} custom-call(bf16[16,3072,128]{2,1,0:T(8,128)(2,1)} %ints.1, bf16[64,768]{1,0:T(8,128)(2,1)} %bitcast.3, bf16[128,512]{1,0:T(8,128)(2,1)} %constant.2.clone.table, s32[2,48]{1,0:T(2,128)} %bitcast.4, s32[2,48]{1,0:T(2,128)} %bitcast.5), custom_call_target="tpu_custom_call" | custom-call | tf_op jit(solution)/shard_map/exchange/pallas_call | solution.py:414
  116.0 2.3 %reshape.3 = f32[384,4,128]{2,1,0:T(4,128)} reshape(f32[4,96,512]{2,1,0:T(8,128)} %exchange.1) | data formatting | bytes 1572864 | tf_op jit(solution)/shard_map/reshape | solution.py:451

commit v3 on v2

v3 whole, which is shorter than its diff:
```python
import functools

import jax
import jax.numpy as jnp
import numpy as np
from jax import lax
from jax.experimental import pallas as pl
from jax.experimental.pallas import tpu as pltpu
from jax.sharding import PartitionSpec as P

BLK = 64
NNZ = 2
MU_DEV = 128
AUX = 16
ROWS = 3072
CHUNK = 384
QUART = 96
WIDTH = 128
KDIM = AUX * WIDTH
MESH = pl.DeviceIdType.MESH
SIGN_ENTRIES = (
    (0, 0, 0, 1),
    (0, 1, 1, 1),
    (0, 2, 2, 1),
    (0, 3, 3, 1),
    (1, 0, 1, -1),
    (1, 1, 0, 1),
    (1, 2, 3, -1),
    (1, 3, 2, 1),
    (2, 0, 2, -1),
    (2, 1, 3, 1),
    (2, 2, 0, 1),
    (2, 3, 1, -1),
    (3, 0, 3, -1),
    (3, 1, 2, -1),
    (3, 2, 1, 1),
    (3, 3, 0, 1),
)


def signed_permutations():
    table = np.zeros((WIDTH, 4, WIDTH), np.float32)
    for r, q, s, sign in SIGN_ENTRIES:
        for i in range(WIDTH // 4):
            table[4 * i + q, r, 4 * i + s] = sign
    return table.reshape(WIDTH, 4 * WIDTH)


def dot_nt(a, b):
    return lax.dot_general(
        a, b, (((1,), (1,)), ((), ())), preferred_element_type=jnp.float32
    )


def kernel(
    ints, coef, table, offs, mask, out,
    win_in, ints_v, G, win, mixed, half, part, partf,
    r1a, r1b, r2a, r2b, quarter, fin, last,
    lsem, gs, gr, ws, wr, s1s, s1r, s2s, s2r, qs, qr, ts, tr,
):
    fit = lax.axis_index("fit")
    b = lax.axis_index("basis")
    yl = lax.axis_index("occ")
    z = fit // 4
    x = fit % 4
    yh = b // 2
    c = b % 2
    oyl = 1 - yl
    partner = 2 * yh + (1 - c)

    def basis_at(k):
        return 2 * ((yh + k // 2) % 2) + (c + k % 2) % 2

    def dev(zz, xx, bb, ll):
        return (zz * 4 + xx, bb, ll)

    def rows(q):
        return pl.ds(pl.multiple_of(q * QUART, QUART), QUART)

    locals_ = [pltpu.make_async_copy(ints.at[:, pl.ds(0, MU_DEV), :], win_in, lsem.at[0])]
    for xx in range(4):
        start = pl.multiple_of((2 * xx + yl) * CHUNK, CHUNK)
        locals_.append(
            pltpu.make_async_copy(
                ints.at[:, pl.ds(start, CHUNK), :], ints_v.at[xx], lsem.at[1 + xx]
            )
        )
    for copy in locals_:
        copy.start()

    for t in range(3):
        G[z, x, yl, c, t] = coef[:, pl.ds(pl.multiple_of(c * CHUNK + t * 128, 128), 128)]

    barrier = pltpu.get_barrier_semaphore()

    def greet(target):
        pl.semaphore_signal(barrier, inc=1, device_id=target, device_id_type=MESH)

    for dz in range(4):
        for k in range(4):
            if dz or k:
                greet(dev((z + dz) % 4, x, basis_at(k), yl))
    for dz in range(4):
        for dx in (1, 2, 3):
            greet(dev((z + dz) % 4, (x + dx) % 4, b, yl))
    greet(dev(z, x, b, oyl))
    greet(dev(z, x, basis_at(2), oyl))
    pl.semaphore_wait(barrier, 29)

    def send(src, dst, ssem, rsem, target):
        copy = pltpu.make_async_remote_copy(
            src_ref=src,
            dst_ref=dst,
            send_sem=ssem,
            recv_sem=rsem,
            device_id=target,
            device_id_type=MESH,
        )
        copy.start()
        return copy

    sent = []


    def gather(phase, n, ref, target):
        copy = send(ref, ref, gs.at[phase, n], gr.at[phase, n], target)
        sent.append(copy)
        return copy

    order = sorted(range(16), key=lambda n: min(n // 4, 4 - n // 4) + min(n % 4, 4 - n % 4))
    direct = {}
    for n in order[1:]:
        target = dev((z + n // 4) % 4, (x + n % 4) % 4, b, yl)
        direct[n] = gather(0, n, G.at[z, x, yl, c], target)
    aside = {}
    onchip = []
    for n in order:
        if n:
            direct[n].wait_recv()
        zz, xx = (z + 4 - n // 4) % 4, (x + 4 - n % 4) % 4
        turn = (yl + zz + xx) % 2
        ref = G.at[zz, xx, yl, c]
        aside[n] = gather(1, n, ref, dev(z, x, 2 * ((yh + turn) % 2) + c, oyl))
        onchip.append(gather(2, n, ref, dev(z, x, partner, yl)))
    for n in order:
        aside[n].wait_recv()
        zz, xx = (z + 4 - n // 4) % 4, (x + 4 - n % 4) % 4
        onchip.append(gather(3, n, G.at[zz, xx, oyl, c], dev(z, x, partner, yl)))
    for copy in onchip:
        copy.wait_recv()
    zp, zm = (z + 1) % 4, (z + 3) % 4
    xp, xm = (x + 1) % 4, (x + 3) % 4

    lane = lax.broadcasted_iota(jnp.int32, (WIDTH, WIDTH), 1)

    def picked(rb):
        sides = []
        for k in range(NNZ):
            off = offs[k, rb]
            keep = mask[k, rb].astype(jnp.float32)
            odd = lax.rem(off, 2).astype(jnp.float32) * keep
            even = keep - odd
            tile = lax.div(off, 2)
            f = lax.div(tile, 6)
            core = lax.div(lax.rem(tile, 6), 3)
            at = (lax.div(f, 4), lax.rem(f, 4))
            got = jnp.concatenate(
                [G[(*at, o, core, lax.rem(tile, 3))] for o in range(2)], axis=0
            ).astype(jnp.float32)
            turned = pltpu.roll(got, 64, 1)
            if k == 0:
                sides.append(got * even + turned * odd)
            else:
                sides.append(got * odd + turned * even)
        return jnp.where(lane < BLK, sides[0], sides[1]).astype(jnp.bfloat16)

    locals_[0].wait()
    for rb in range(MU_DEV // BLK):
        slab = win_in[:, rb * BLK : (rb + 1) * BLK, :].reshape(AUX * BLK, WIDTH)
        got = dot_nt(slab, picked(rb)).astype(jnp.bfloat16)
        for p in range(AUX):
            win[b, rb * BLK : (rb + 1) * BLK, p * WIDTH : (p + 1) * WIDTH] = got[
                p * BLK : (p + 1) * BLK
            ]
    window = [
        send(win.at[b], win.at[b], ws.at[0], wr.at[0], dev(z, x, partner, yl)),
        send(win.at[b], win.at[b], ws.at[1], wr.at[1], dev(z, x, basis_at(2), oyl)),
    ]
    sent.extend(window)

    for xx in range(4):
        locals_[1 + xx].wait()

    @pl.loop(0, 24)
    def _(i):
        xx = i // 6
        r = i % 6
        slab = ints_v[xx, :, pl.ds(pl.multiple_of(r * BLK, BLK), BLK), :]
        weights = picked((2 * xx + yl) * 6 + r)
        got = dot_nt(slab.reshape(AUX * BLK, WIDTH), weights).astype(jnp.bfloat16)
        at = pl.ds(pl.multiple_of(i * BLK, BLK), BLK)
        for p in range(AUX):
            half[at, p * WIDTH : (p + 1) * WIDTH] = got[p * BLK : (p + 1) * BLK]

    def mix(k):
        bb = basis_at(k)

        @pl.loop(0, AUX, unroll=4)
        def _(p):
            at = pl.ds(pl.multiple_of(p * WIDTH, WIDTH), WIDTH)
            got = jnp.dot(win[bb, :, at], table[...], preferred_element_type=jnp.float32)
            got = got.astype(jnp.bfloat16)
            for r in range(4):
                mixed[r // 2, (r % 2) * 128 : (r % 2) * 128 + 128, at] = got[
                    :, r * WIDTH : (r + 1) * WIDTH
                ]

    def dots(k, h):
        @pl.loop(0, 2)
        def _(i):
            at = pl.ds(pl.multiple_of(i * 2 * CHUNK, 2 * CHUNK), 2 * CHUNK)
            got = dot_nt(half[at, :], mixed[h]).reshape(2, CHUNK, 256)
            two = pl.ds(2 * i, 2)
            partf[k, h, two] = got
            part[k, h, two] = got.astype(jnp.bfloat16)

    def piece(ref, k, h, q, s):
        if h == 0:
            return ref.at[k, h, q, pl.ds(s * 192, 192)]
        return ref.at[k, h, :, pl.ds(pl.multiple_of(q * QUART + s * 48, 16), 48)]

    def recv_one(k, h, side):
        return (r1a if h == 0 else r1b).at[k, side]

    def recv_two(k, h, side, s):
        return (r2a if h == 0 else r2b).at[k, side, s]

    flights = {}

    def ring(axis):
        if axis == 0:
            return x, lambda d: dev(z, (x + d) % 4, b, yl)
        return z, lambda d: dev((z + d) % 4, x, b, yl)

    def launch(k, h):
        me, peer = ring(h)
        got = {}
        for side in range(2):
            got["one", side] = send(
                piece(part, k, h, (me + 2) % 4, side), recv_one(k, h, side),
                s1s.at[k, h, side], s1r.at[k, h, side], peer(1 + 2 * side),
            )
        for side in range(2):
            got["two", side, 1 - side] = send(
                piece(part, k, h, (me + 1 + 2 * side) % 4, 1 - side),
                recv_two(k, h, side, 1 - side),
                s2s.at[k, h, side, 1 - side], s2r.at[k, h, side, 1 - side],
                peer(1 + 2 * side),
            )
        flights[k, h] = got

    def relay(k, h):
        me, peer = ring(h)
        got = flights[k, h]
        for side in range(2):
            got["one", side].wait_recv()
            at = (me + 1 + 2 * side) % 4
            total = piece(partf, k, h, at, side)[...]
            total += recv_one(k, h, side)[...].astype(jnp.float32)
            piece(part, k, h, at, side)[...] = total.astype(jnp.bfloat16)
            got["two", side, side] = send(
                piece(part, k, h, at, side), recv_two(k, h, side, side),
                s2s.at[k, h, side, side], s2r.at[k, h, side, side], peer(1 + 2 * side),
            )

    def own(ref, k, h, q):
        return ref.at[k, h, x, rows(q)] if h == 0 else ref.at[k, h, q, rows(z)]

    def collect(k, h):
        me, _ = ring(h)
        got = flights[k, h]
        for s in range(2):
            got["two", 0, s].wait_recv()
            got["two", 1, s].wait_recv()
            total = piece(partf, k, h, me, s)[...]
            total += recv_two(k, h, 0, s)[...].astype(jnp.float32)
            total += recv_two(k, h, 1, s)[...].astype(jnp.float32)
            piece(partf, k, h, me, s)[...] = total
            piece(part, k, h, me, s)[...] = total.astype(jnp.bfloat16)
        me, peer = ring(1 - h)
        for d in (2, 1, 3):
            got["far", d] = send(
                own(part, k, h, (me + d) % 4), quarter.at[k, h, d - 1],
                qs.at[k, h, d - 1], qr.at[k, h, d - 1], peer(d),
            )

    def finish(k, h):
        me, _ = ring(1 - h)
        got = flights[k, h]
        total = own(partf, k, h, me)[...]
        for d in (1, 3, 2):
            got["far", d].wait_recv()
            total += quarter[k, h, d - 1].astype(jnp.float32)
        fin[k, :, h * 256 : (h + 1) * 256] = total.astype(jnp.bfloat16)

    finals = []

    def deliver(k):
        target = dev(b, x, basis_at(k), yl)
        if k == 0:
            same = z == b

            @pl.when(same)
            def _():
                pltpu.make_async_copy(fin.at[k], last.at[z], tr.at[z]).start()

            @pl.when(jnp.logical_not(same))
            def _():
                send(fin.at[k], last.at[z], ts.at[k], tr.at[z], target)
        else:
            finals.append(send(fin.at[k], last.at[z], ts.at[k], tr.at[z], target))

    order = (0, 2, 3, 1)
    forward = None
    for i, k in enumerate(order):
        if k == 2:
            window[1].wait_recv()
            other = win.at[basis_at(2)]
            forward = send(other, other, ws.at[2], wr.at[2], dev(z, x, partner, yl))
            sent.append(forward)
        elif k == 3:
            forward.wait_recv()
        elif k == 1:
            window[0].wait_recv()
        mix(k)
        for h in (1, 0):
            dots(k, h)
            if i >= 1:
                relay(order[i - 1], h)
            launch(k, h)
            if i >= 2:
                collect(order[i - 2], h)
    for h in range(2):
        relay(order[3], h)
    for h in range(2):
        collect(order[2], h)
    for i in range(2):
        for h in range(2):
            finish(order[i], h)
        deliver(order[i])
    for h in range(2):
        collect(order[3], h)
    for i in range(2, 4):
        for h in range(2):
            finish(order[i], h)
        deliver(order[i])

    for q in range(4):
        pltpu.make_async_copy(fin.at[0], last.at[q], tr.at[q]).wait()
        for r in range(4):
            out[pl.ds(q * CHUNK + r, QUART, stride=4), :] = last[
                q, :, r * MU_DEV : (r + 1) * MU_DEV
            ].astype(jnp.float32)
    for copy in sent:
        copy.wait_send()
    for got in flights.values():
        for copy in got.values():
            copy.wait_send()

    @pl.when(z != b)
    def _():
        pltpu.make_async_remote_copy(
            src_ref=fin.at[0], dst_ref=last.at[z], send_sem=ts.at[0], recv_sem=tr.at[z],
            device_id=dev(b, x, b, yl), device_id_type=MESH,
        ).wait_send()

    for copy in finals:
        copy.wait_send()


def shards(ints, coeffs, offsets, mask):
    table = jnp.asarray(signed_permutations(), jnp.bfloat16)
    bf16, f32 = jnp.bfloat16, jnp.float32
    vmem = pl.BlockSpec(memory_space=pltpu.VMEM)
    smem = pl.BlockSpec(memory_space=pltpu.SMEM)
    dma = pltpu.SemaphoreType.DMA
    result = pl.pallas_call(
        kernel,
        out_shape=jax.ShapeDtypeStruct((4 * CHUNK, MU_DEV), f32),
        in_specs=[pl.BlockSpec(memory_space=pl.ANY), vmem, vmem, smem, smem],
        out_specs=vmem,
        scratch_shapes=[
            pltpu.VMEM((AUX, MU_DEV, WIDTH), bf16),
            pltpu.VMEM((4, AUX, CHUNK, WIDTH), bf16),
            pltpu.VMEM((4, 4, 2, 2, 3, 64, 128), bf16),
            pltpu.VMEM((4, MU_DEV, KDIM), bf16),
            pltpu.VMEM((2, 256, KDIM), bf16),
            pltpu.VMEM((4 * CHUNK, KDIM), bf16),
            pltpu.VMEM((4, 2, 4, CHUNK, 256), bf16),
            pltpu.VMEM((4, 2, 4, CHUNK, 256), f32),
            pltpu.VMEM((4, 2, 192, 256), bf16),
            pltpu.VMEM((4, 2, 4, 48, 256), bf16),
            pltpu.VMEM((4, 2, 2, 192, 256), bf16),
            pltpu.VMEM((4, 2, 2, 4, 48, 256), bf16),
            pltpu.VMEM((4, 2, 3, QUART, 256), bf16),
            pltpu.VMEM((4, QUART, 512), bf16),
            pltpu.VMEM((4, QUART, 512), bf16),
            dma((5,)),
            dma((4, 16)),
            dma((4, 16)),
            dma((3,)),
            dma((3,)),
            dma((4, 2, 2)),
            dma((4, 2, 2)),
            dma((4, 2, 2, 2)),
            dma((4, 2, 2, 2)),
            dma((4, 2, 3)),
            dma((4, 2, 3)),
            dma((4,)),
            dma((4,)),
        ],
        compiler_params=pltpu.CompilerParams(
            collective_id=0, has_side_effects=True, vmem_limit_bytes=60 * 1024 * 1024
        ),
        name="exchange",
    )(ints, coeffs.T, table, offsets.T, mask.T)
    return result.reshape(CHUNK, 4, MU_DEV)


def solution(mesh):
    return jax.shard_map(
        shards,
        mesh=mesh,
        in_specs=(P("fit", "basis", None), P("fit", "occ"), P("basis", None), P("basis", None)),
        out_specs=P(("fit", "occ"), None, "basis"),
        check_vma=False,
    )
```

time: 118 us -> 92.3 us (0.78)
  the two profiles are of different devices: /device:TPU:25 before, /device:TPU:1 now
where the time goes in v3:
time: 92.3 us; the launch traced here: 92.2 us
  Pallas kernels  90.1 us (98%)
  local copies, waits for them, and re-layouts  2.06 us (2%)
    pallas_call x1, Pallas kernels, shards(): pl.pallas_call(kernel, out_shape=jax.ShapeDtypeStruct((4 * CHUNK, MU_DEV)...  90.1 us
    unnamed x1, local copies, waits for them, and re-layouts  2.06 us

profile of v3, /device:TPU:1, one launch (start us, length us, event | category | flops | bytes accessed | tf_op | source)
XLA Modules:
  0.0 92.2 jit_solution(14378675049534172122)
XLA Ops:
  0.0 90.1 %exchange.1 = f32[1536,128]{1,0:T(8,128)} custom-call(bf16[16,3072,128]{2,1,0:T(8,128)(2,1)} %ints.1, bf16[64,768]{1,0:T(8,128)(2,1)} %bitcast.5, bf16[128,512]{1,0:T(8,128)(2,1)} %constant.2.clone.table, s32[2,48]{1,0:T(2,128)} %bitcast.6, s32[2,48]{1,0:T(2,128)} %bitcast.7), custom_call_target="tpu_custom_call" | custom-call | tf_op jit(solution)/shard_map/exchange/pallas_call | solution.py:387
  90.1 2.1 %copy.7 = f32[384,4,128]{2,1,0:T(4,128)} copy(f32[384,4,128]{2,1,0:T(4,128)} %bitcast.4) | data formatting | bytes 1572864

commit v4 on v3

--- a/solution.py
+++ b/solution.py
@@ -96,16 +96,13 @@
     def greet(target):
         pl.semaphore_signal(barrier, inc=1, device_id=target, device_id_type=MESH)
 
-    for dz in range(4):
-        for k in range(4):
-            if dz or k:
-                greet(dev((z + dz) % 4, x, basis_at(k), yl))
-    for dz in range(4):
-        for dx in (1, 2, 3):
-            greet(dev((z + dz) % 4, (x + dx) % 4, b, yl))
+    for d in (1, 2, 3):
+        greet(dev(z, (x + d) % 4, b, yl))
+        greet(dev((z + d) % 4, x, b, yl))
     greet(dev(z, x, b, oyl))
     greet(dev(z, x, basis_at(2), oyl))
-    pl.semaphore_wait(barrier, 29)
+    greet(dev(z, x, partner, yl))
+    pl.semaphore_wait(barrier, 9)
 
     def send(src, dst, ssem, rsem, target):
         copy = pltpu.make_async_remote_copy(
@@ -122,30 +119,74 @@
     sent = []
 
 
-    def gather(phase, n, ref, target):
-        copy = send(ref, ref, gs.at[phase, n], gr.at[phase, n], target)
+    near = (1, 3, 2)
+    colors = (0, 1)
+
+    def half_piece(color, first, second, o):
+        dx, dz = (first, second) if color == 0 else (second, first)
+        at = (z + 4 - dz) % 4, (x + 4 - dx) % 4
+        return G.at[(*at, o, c)].at[:, pl.ds(32 * color, 32), :]
+
+    def half_group(color, second, o):
+        if color == 0:
+            return G.at[(z + 4 - second) % 4, :, o, c, :, pl.ds(0, 32), :]
+        return G.at[:, (x + 4 - second) % 4, o, c, :, pl.ds(32, 32), :]
+
+    def along(axis, d):
+        return dev(z, (x + d) % 4, b, yl) if axis == 0 else dev((z + d) % 4, x, b, yl)
+
+    def gather(phase, color, m, d, ref, target):
+        n = m * 4 + d
+        copy = send(ref, ref, gs.at[phase, color, n], gr.at[phase, color, n], target)
         sent.append(copy)
         return copy
 
-    order = sorted(range(16), key=lambda n: min(n // 4, 4 - n // 4) + min(n % 4, 4 - n % 4))
-    direct = {}
-    for n in order[1:]:
-        target = dev((z + n // 4) % 4, (x + n % 4) % 4, b, yl)
-        direct[n] = gather(0, n, G.at[z, x, yl, c], target)
-    aside = {}
-    onchip = []
-    for n in order:
-        if n:
-            direct[n].wait_recv()
-        zz, xx = (z + 4 - n // 4) % 4, (x + 4 - n % 4) % 4
-        turn = (yl + zz + xx) % 2
-        ref = G.at[zz, xx, yl, c]
-        aside[n] = gather(1, n, ref, dev(z, x, 2 * ((yh + turn) % 2) + c, oyl))
-        onchip.append(gather(2, n, ref, dev(z, x, partner, yl)))
-    for n in order:
-        aside[n].wait_recv()
-        zz, xx = (z + 4 - n // 4) % 4, (x + 4 - n % 4) % 4
-        onchip.append(gather(3, n, G.at[zz, xx, oyl, c], dev(z, x, partner, yl)))
+    one, two, side_y, onchip = {}, {}, {}, []
+
+    def second_stage(color, m):
+        for d in near:
+            two[color, m, d] = gather(
+                1, color, m, d, half_piece(color, m, 0, yl), along(1 - color, d)
+            )
+
+    def pair(color, d, o, phase):
+        onchip.append(
+            gather(phase, color, 0, d, half_group(color, d, o), dev(z, x, partner, yl))
+        )
+
+    def outward(color, m, d):
+        turn = (yl + color) % 2
+        side_y[color, m, d] = gather(
+            2, color, m, d, half_piece(color, m, d, yl),
+            dev(z, x, 2 * ((yh + turn) % 2) + c, oyl),
+        )
+
+    for d in near:
+        for color in colors:
+            one[color, d] = gather(
+                0, color, 0, d, half_piece(color, 0, 0, yl), along(color, d)
+            )
+    for color in colors:
+        second_stage(color, 0)
+        outward(color, 0, 0)
+    for m in near:
+        for color in colors:
+            one[color, m].wait_recv()
+            second_stage(color, m)
+            outward(color, m, 0)
+    for m in (0, 1, 3, 2):
+        for d in near:
+            for color in colors:
+                two[color, m, d].wait_recv()
+                outward(color, m, d)
+    for d in (0, 1, 3, 2):
+        for color in colors:
+            pair(color, d, yl, 3)
+    for d in (0, 1, 3, 2):
+        for color in colors:
+            for m in (0, 1, 3, 2):
+                side_y[color, m, d].wait_recv()
+            pair(color, d, oyl, 4)
     for copy in onchip:
         copy.wait_recv()
     zp, zm = (z + 1) % 4, (z + 3) % 4
@@ -191,7 +232,7 @@
     for xx in range(4):
         locals_[1 + xx].wait()
 
-    @pl.loop(0, 24)
+    @pl.loop(0, 24, unroll=8)
     def _(i):
         xx = i // 6
         r = i % 6
@@ -320,7 +361,7 @@
         else:
             finals.append(send(fin.at[k], last.at[z], ts.at[k], tr.at[z], target))
 
-    order = (0, 2, 3, 1)
+    order = (0, 1, 2, 3)
     forward = None
     for i, k in enumerate(order):
         if k == 2:
@@ -406,8 +447,8 @@
             pltpu.VMEM((4, QUART, 512), bf16),
             pltpu.VMEM((4, QUART, 512), bf16),
             dma((5,)),
-            dma((4, 16)),
-            dma((4, 16)),
+            dma((5, 2, 16)),
+            dma((5, 2, 16)),
             dma((3,)),
             dma((3,)),
             dma((4, 2, 2)),

time: 92.3 us -> 82.5 us (0.89)
  the two profiles are of different devices: /device:TPU:1 before, /device:TPU:25 now
where the time goes in v4:
time: 82.5 us; the launch traced here: 82.1 us
  Pallas kernels  80 us (97%)
  local copies, waits for them, and re-layouts  2.06 us (2%)
    pallas_call x1, Pallas kernels, shards(): pl.pallas_call(kernel, out_shape=jax.ShapeDtypeStruct((4 * CHUNK, MU_DEV)...  80 us
    unnamed x1, local copies, waits for them, and re-layouts  2.06 us

profile of v4, /device:TPU:25, one launch (start us, length us, event | category | flops | bytes accessed | tf_op | source)
XLA Modules:
  0.0 82.1 jit_solution(7950054926262917822)
XLA Ops:
  0.0 80.0 %exchange.1 = f32[1536,128]{1,0:T(8,128)} custom-call(bf16[16,3072,128]{2,1,0:T(8,128)(2,1)} %ints.1, bf16[64,768]{1,0:T(8,128)(2,1)} %bitcast.5, bf16[128,512]{1,0:T(8,128)(2,1)} %constant.2.clone.table, s32[2,48]{1,0:T(2,128)} %bitcast.6, s32[2,48]{1,0:T(2,128)} %bitcast.7), custom_call_target="tpu_custom_call" | custom-call | tf_op jit(solution)/shard_map/exchange/pallas_call | solution.py:428
  80.0 2.1 %copy.7 = f32[384,4,128]{2,1,0:T(4,128)} copy(f32[384,4,128]{2,1,0:T(4,128)} %bitcast.4) | data formatting | bytes 1572864

commit v5 on v4

--- a/solution.py
+++ b/solution.py
@@ -18,6 +18,11 @@
 WIDTH = 128
 KDIM = AUX * WIDTH
 MESH = pl.DeviceIdType.MESH
+UNITS = tuple((k, h) for k in range(4) for h in range(2))
+X_FIRST = ((0, 0), (1, 0), (2, 0), (3, 0))
+N_X = len(X_FIRST)
+N_Z = len(UNITS) - N_X
+H_ORDER = (0, 1)
 SIGN_ENTRIES = (
     (0, 0, 0, 1),
     (0, 1, 1, 1),
@@ -246,7 +251,7 @@
     def mix(k):
         bb = basis_at(k)
 
-        @pl.loop(0, AUX, unroll=4)
+        @pl.loop(0, AUX, unroll=16)
         def _(p):
             at = pl.ds(pl.multiple_of(p * WIDTH, WIDTH), WIDTH)
             got = jnp.dot(win[bb, :, at], table[...], preferred_element_type=jnp.float32)
@@ -265,16 +270,23 @@
             partf[k, h, two] = got
             part[k, h, two] = got.astype(jnp.bfloat16)
 
+    def color_of(k, h):
+        return 0 if (k, h) in X_FIRST else 1
+
+    def slot(k, h):
+        same = [u for u in UNITS if color_of(*u) == color_of(k, h)]
+        return same.index((k, h))
+
     def piece(ref, k, h, q, s):
-        if h == 0:
+        if color_of(k, h) == 0:
             return ref.at[k, h, q, pl.ds(s * 192, 192)]
         return ref.at[k, h, :, pl.ds(pl.multiple_of(q * QUART + s * 48, 16), 48)]
 
     def recv_one(k, h, side):
-        return (r1a if h == 0 else r1b).at[k, side]
+        return (r1a, r1b)[color_of(k, h)].at[slot(k, h), side]
 
     def recv_two(k, h, side, s):
-        return (r2a if h == 0 else r2b).at[k, side, s]
+        return (r2a, r2b)[color_of(k, h)].at[slot(k, h), side, s]
 
     flights = {}
 
@@ -284,7 +296,7 @@
         return z, lambda d: dev((z + d) % 4, x, b, yl)
 
     def launch(k, h):
-        me, peer = ring(h)
+        me, peer = ring(color_of(k, h))
         got = {}
         for side in range(2):
             got["one", side] = send(
@@ -301,7 +313,7 @@
         flights[k, h] = got
 
     def relay(k, h):
-        me, peer = ring(h)
+        me, peer = ring(color_of(k, h))
         got = flights[k, h]
         for side in range(2):
             got["one", side].wait_recv()
@@ -315,10 +327,12 @@
             )
 
     def own(ref, k, h, q):
-        return ref.at[k, h, x, rows(q)] if h == 0 else ref.at[k, h, q, rows(z)]
+        if color_of(k, h) == 0:
+            return ref.at[k, h, x, rows(q)]
+        return ref.at[k, h, q, rows(z)]
 
     def collect(k, h):
-        me, _ = ring(h)
+        me, _ = ring(color_of(k, h))
         got = flights[k, h]
         for s in range(2):
             got["two", 0, s].wait_recv()
@@ -328,7 +342,7 @@
             total += recv_two(k, h, 1, s)[...].astype(jnp.float32)
             piece(partf, k, h, me, s)[...] = total
             piece(part, k, h, me, s)[...] = total.astype(jnp.bfloat16)
-        me, peer = ring(1 - h)
+        me, peer = ring(1 - color_of(k, h))
         for d in (2, 1, 3):
             got["far", d] = send(
                 own(part, k, h, (me + d) % 4), quarter.at[k, h, d - 1],
@@ -336,7 +350,7 @@
             )
 
     def finish(k, h):
-        me, _ = ring(1 - h)
+        me, _ = ring(1 - color_of(k, h))
         got = flights[k, h]
         total = own(partf, k, h, me)[...]
         for d in (1, 3, 2):
@@ -374,7 +388,7 @@
         elif k == 1:
             window[0].wait_recv()
         mix(k)
-        for h in (1, 0):
+        for h in H_ORDER:
             dots(k, h)
             if i >= 1:
                 relay(order[i - 1], h)
@@ -385,13 +399,9 @@
         relay(order[3], h)
     for h in range(2):
         collect(order[2], h)
-    for i in range(2):
-        for h in range(2):
-            finish(order[i], h)
-        deliver(order[i])
     for h in range(2):
         collect(order[3], h)
-    for i in range(2, 4):
+    for i in range(4):
         for h in range(2):
             finish(order[i], h)
         deliver(order[i])
@@ -439,10 +449,10 @@
             pltpu.VMEM((4 * CHUNK, KDIM), bf16),
             pltpu.VMEM((4, 2, 4, CHUNK, 256), bf16),
             pltpu.VMEM((4, 2, 4, CHUNK, 256), f32),
-            pltpu.VMEM((4, 2, 192, 256), bf16),
-            pltpu.VMEM((4, 2, 4, 48, 256), bf16),
-            pltpu.VMEM((4, 2, 2, 192, 256), bf16),
-            pltpu.VMEM((4, 2, 2, 4, 48, 256), bf16),
+            pltpu.VMEM((N_X, 2, 192, 256), bf16),
+            pltpu.VMEM((N_Z, 2, 4, 48, 256), bf16),
+            pltpu.VMEM((N_X, 2, 2, 192, 256), bf16),
+            pltpu.VMEM((N_Z, 2, 2, 4, 48, 256), bf16),
             pltpu.VMEM((4, 2, 3, QUART, 256), bf16),
             pltpu.VMEM((4, QUART, 512), bf16),
             pltpu.VMEM((4, QUART, 512), bf16),

time: 82.5 us -> 79.2 us (0.960)
  Pallas kernels: 80 us -> 76.9 us
    pallas_call x1, Pallas kernels: 80 us -> 76.9 us  [shards(): pl.pallas_call(kernel, out_shape=jax.ShapeDtypeStruct((4 * CHUNK, MU_DEV)...]
where the time goes in v5:
time: 79.2 us; the launch traced here: 78.9 us
  Pallas kernels  76.9 us (97%)
  local copies, waits for them, and re-layouts  2.06 us (3%)
    pallas_call x1, Pallas kernels, shards(): pl.pallas_call(kernel, out_shape=jax.ShapeDtypeStruct((4 * CHUNK, MU_DEV)...  76.9 us
    unnamed x1, local copies, waits for them, and re-layouts  2.06 us

profile of v5, /device:TPU:25, one launch (start us, length us, event | category | flops | bytes accessed | tf_op | source)
XLA Modules:
  0.0 78.9 jit_solution(17334997190029423329)
XLA Ops:
  0.0 76.9 %exchange.1 = f32[1536,128]{1,0:T(8,128)} custom-call(bf16[16,3072,128]{2,1,0:T(8,128)(2,1)} %ints.1, bf16[64,768]{1,0:T(8,128)(2,1)} %bitcast.5, bf16[128,512]{1,0:T(8,128)(2,1)} %constant.2.clone.table, s32[2,48]{1,0:T(2,128)} %bitcast.6, s32[2,48]{1,0:T(2,128)} %bitcast.7), custom_call_target="tpu_custom_call" | custom-call | tf_op jit(solution)/shard_map/exchange/pallas_call | solution.py:438
  76.9 2.1 %copy.7 = f32[384,4,128]{2,1,0:T(4,128)} copy(f32[384,4,128]{2,1,0:T(4,128)} %bitcast.4) | data formatting | bytes 1572864

commit v6 on v5

--- a/solution.py
+++ b/solution.py
@@ -248,18 +248,17 @@
         for p in range(AUX):
             half[at, p * WIDTH : (p + 1) * WIDTH] = got[p * BLK : (p + 1) * BLK]
 
-    def mix(k):
+    def mix(k, h):
         bb = basis_at(k)
 
         @pl.loop(0, AUX, unroll=16)
         def _(p):
             at = pl.ds(pl.multiple_of(p * WIDTH, WIDTH), WIDTH)
-            got = jnp.dot(win[bb, :, at], table[...], preferred_element_type=jnp.float32)
+            signs = table[:, h * 256 : (h + 1) * 256]
+            got = jnp.dot(win[bb, :, at], signs, preferred_element_type=jnp.float32)
             got = got.astype(jnp.bfloat16)
-            for r in range(4):
-                mixed[r // 2, (r % 2) * 128 : (r % 2) * 128 + 128, at] = got[
-                    :, r * WIDTH : (r + 1) * WIDTH
-                ]
+            for r in range(2):
+                mixed[h, r * 128 : (r + 1) * 128, at] = got[:, r * WIDTH : (r + 1) * WIDTH]
 
     def dots(k, h):
         @pl.loop(0, 2)
@@ -387,8 +386,8 @@
             forward.wait_recv()
         elif k == 1:
             window[0].wait_recv()
-        mix(k)
         for h in H_ORDER:
+            mix(k, h)
             dots(k, h)
             if i >= 1:
                 relay(order[i - 1], h)

time: 79.2 us -> 79.3 us (level)
  no operation moved by 1% of the time
where the time goes in v6:
time: 79.3 us; the launch traced here: 78.9 us
  Pallas kernels  76.9 us (97%)
  local copies, waits for them, and re-layouts  2.06 us (3%)
    pallas_call x1, Pallas kernels, shards(): pl.pallas_call(kernel, out_shape=jax.ShapeDtypeStruct((4 * CHUNK, MU_DEV)...  76.9 us
    unnamed x1, local copies, waits for them, and re-layouts  2.06 us

profile of v6, /device:TPU:25, one launch (start us, length us, event | category | flops | bytes accessed | tf_op | source)
XLA Modules:
  0.0 78.9 jit_solution(7625067961268999683)
XLA Ops:
  0.0 76.9 %exchange.1 = f32[1536,128]{1,0:T(8,128)} custom-call(bf16[16,3072,128]{2,1,0:T(8,128)(2,1)} %ints.1, bf16[64,768]{1,0:T(8,128)(2,1)} %bitcast.5, bf16[128,512]{1,0:T(8,128)(2,1)} %constant.2.clone.table, s32[2,48]{1,0:T(2,128)} %bitcast.6, s32[2,48]{1,0:T(2,128)} %bitcast.7), custom_call_target="tpu_custom_call" | custom-call | tf_op jit(solution)/shard_map/exchange/pallas_call | solution.py:437
  76.9 2.1 %copy.7 = f32[384,4,128]{2,1,0:T(4,128)} copy(f32[384,4,128]{2,1,0:T(4,128)} %bitcast.4) | data formatting | bytes 1572864
